TPU v7x, 32 devices: a whole 2x2x4 slice. The times are simulated.
32 devices in a mesh: group: 4 (over x, core), blk: 8 (over z, y).
Axes of the slice: x: 2, y: 2, z: 4, core: 2. Of those that a mesh axis runs over, the one named last changes fastest.
Arguments:
- vertex: float32 [32768, 256], P(('group', 'blk')), may hold values from -1.5 to 1.5
- vertex_state: float32 [32768], P(('group', 'blk')), may hold values from 0.1 to 1
- context: float32 [16384, 256], P(('group', 'blk')), may hold values from -1.5 to 1.5
- context_state: float32 [16384], P(('group', 'blk')), may hold values from 0.1 to 1
- tile_weights: bfloat16 [4, 8, 4, 6, 3, 128, 128], P('group', 'blk'), may hold values from 0.049804688 to 2
- tile_rows: int32 [4, 8, 4, 6, 3], P('group', 'blk'), may hold values from 0 to 7
- tile_cols: int32 [4, 8, 4, 6, 3], P('group', 'blk'), may hold values from 0 to 3
- tile_counts: int32 [4, 8, 4, 6], P('group', 'blk'), may hold values from 1 to 3, as said below
- negatives: int32 [4, 8, 6, 8, 2], P('group', 'blk'), may hold values from 0 to 3
Outputs:
- vertex_out: float32 [32768, 256], P(('group', 'blk'))
- vertex_state_out: float32 [32768], P(('group', 'blk'))
- context_out: float32 [16384, 256], P(('group', 'blk'))
- context_state_out: float32 [16384], P(('group', 'blk'))
Inputs may be any that keep to these rules, and one draw needn't show every extreme that they name: `tile_counts`: at each stop and each index of blk some destination of the group receives 3 used slots from every walk owner.
All inputs are finite; a program needn't handle non-finite values.
Results may differ from a plain program's by a relative error of at most 0.0049.
Values may be sent and summed in bfloat16 or wider, within the bound.
A program may use at most 64 MiB of HBM per device.

v0:
```python
import functools

import jax
import jax.numpy as jnp
from jax import lax
from jax.experimental import pallas as pl
from jax.experimental.pallas import tpu as pltpu
from jax.sharding import PartitionSpec as P

LEARNING = 0.1
NEG_WEIGHT = 0.5
MESH = pl.DeviceIdType.MESH
SUB = 16


def eye_mask(tile):
    return lax.broadcasted_iota(jnp.int32, (tile, tile), 0) == lax.broadcasted_iota(
        jnp.int32, (tile, tile), 1
    )


def to_column(row):
    tile = row.shape[1]
    return jnp.sum(jnp.where(eye_mask(tile), row, 0.0), axis=1, keepdims=True)


def to_row(column):
    tile = column.shape[0]
    return jnp.sum(jnp.where(eye_mask(tile), column, 0.0), axis=0, keepdims=True)


def kernel(
    sizes,
    vertex_ref,
    vstate_ref,
    context_ref,
    cstate_ref,
    codes_ref,
    negs_ref,
    weights_hbm,
    vout,
    vsout,
    cout,
    csout,
    vb,
    vcol,
    held,
    outgo,
    held_state,
    out_state,
    c32,
    gbuf,
    wagg,
    wbuf,
    codebuf,
    code16,
    hop_send,
    hop_recv,
    st_send,
    st_recv,
    w_send,
    w_recv,
    code_send,
    code_recv,
    own_sem,
    own_code_sem,
):
    n_group, n_blk, steps, cap, row_tiles, ctx_tiles, tile = sizes
    group = lax.axis_index("group")
    blk = lax.axis_index("blk")
    right = lax.rem(blk + 1, n_blk)
    left = lax.rem(blk + n_blk - 1, n_blk)

    def peer(j):
        return lax.rem(group + j, n_group)

    def code_copy(j):
        return pltpu.make_async_remote_copy(
            src_ref=codes_ref.at[peer(j)],
            dst_ref=codebuf.at[j],
            send_sem=code_send.at[j],
            recv_sem=code_recv.at[j],
            device_id={"group": peer(j)},
            device_id_type=MESH,
        )

    def weight_copy(stop, j):
        return pltpu.make_async_remote_copy(
            src_ref=weights_hbm.at[peer(j), stop],
            dst_ref=wbuf.at[stop, j],
            send_sem=w_send.at[stop, j],
            recv_sem=w_recv.at[stop, j],
            device_id={"group": peer(j)},
            device_id_type=MESH,
        )

    def own_copy(stop):
        return pltpu.make_async_copy(
            weights_hbm.at[group, stop], wbuf.at[stop, 0], own_sem.at[stop]
        )

    def own_code():
        return pltpu.make_async_copy(codes_ref.at[group], codebuf.at[0], own_code_sem)

    def hop_copy(stop, c):
        return pltpu.make_async_remote_copy(
            src_ref=outgo.at[stop, c],
            dst_ref=held.at[stop, c],
            send_sem=hop_send.at[stop, c],
            recv_sem=hop_recv.at[stop, c],
            device_id={"blk": right},
            device_id_type=MESH,
        )

    def state_copy(stop, c):
        return pltpu.make_async_remote_copy(
            src_ref=out_state.at[stop, c],
            dst_ref=held_state.at[stop, c],
            send_sem=st_send.at[stop, c],
            recv_sem=st_recv.at[stop, c],
            device_id={"blk": right},
            device_id_type=MESH,
        )

    barrier = pltpu.get_barrier_semaphore()
    pl.semaphore_signal(barrier, inc=1, device_id={"blk": left}, device_id_type=MESH)
    for j in range(1, n_group):
        pl.semaphore_signal(
            barrier, inc=1, device_id={"group": peer(j)}, device_id_type=MESH
        )
    own_code().start()
    for stop in range(steps):
        own_copy(stop).start()
    pl.semaphore_wait(barrier, n_group)

    for j in range(1, n_group):
        code_copy(j).start()
    for stop in range(steps):
        for j in range(1, n_group):
            weight_copy(stop, j).start()

    for r in range(row_tiles):
        rows = slice(r * tile, (r + 1) * tile)
        vb[rows, :] = vertex_ref[rows, :].astype(jnp.bfloat16)
        vout[rows, :] = vertex_ref[rows, :]
        vcol[rows, :] = to_column(vstate_ref[r : r + 1, :])
    for c in range(ctx_tiles):
        held[0, c] = context_ref[c].astype(jnp.bfloat16)
        c32[c] = context_ref[c]
        held_state[0, c] = cstate_ref[c]

    own_code().wait()
    for j in range(1, n_group):
        code_copy(j).wait_recv()
    for j in range(n_group):

        def spread(k, _, j=j):
            code16[j, k] = jnp.broadcast_to(codebuf[j, k], (SUB, tile)).astype(jnp.bfloat16)
            return 0

        lax.fori_loop(0, steps * cap, spread, 0)

    pairs = row_tiles * ctx_tiles
    half = tile // SUB

    def one_stop(s, _):
        own_copy(s).wait()
        for j in range(1, n_group):
            weight_copy(s, j).wait_recv()

        def one_pair(p, _):
            acc = jnp.zeros((half, SUB, tile), jnp.bfloat16)
            here = p.astype(jnp.float32).astype(jnp.bfloat16)
            for j in range(n_group):
                for k in range(cap):
                    hit = jnp.where(
                        code16[j, s * cap + k].astype(jnp.float32) == p.astype(jnp.float32),
                        1.0,
                        0.0,
                    ).astype(jnp.bfloat16)
                    acc = acc + wbuf[s, j, k] * hit[None]
            wagg[p] = acc.reshape(tile, tile)
            return 0

        lax.fori_loop(0, pairs, one_pair, 0)

        for c in range(ctx_tiles):

            @pl.when(s > 0)
            def _():
                hop_copy(s, c).wait_recv()
                state_copy(s, c).wait_recv()
                c32[c] = held[s, c].astype(jnp.float32)

            ctx = held[s, c]
            grad = jnp.zeros(ctx.shape, jnp.float32)
            for r in range(row_tiles):
                rows = slice(r * tile, (r + 1) * tile)
                logits = lax.dot_general(
                    vb[rows, :],
                    ctx,
                    (((1,), (1,)), ((), ())),
                    preferred_element_type=jnp.float32,
                )
                weight = wagg[c * row_tiles + r].astype(jnp.float32)
                scale = 0.5 * (weight + negs_ref[s, c * row_tiles + r])
                g = scale * (1.0 + jnp.tanh(0.5 * logits)) - weight
                g = g.astype(jnp.bfloat16)
                gbuf[rows, c * tile : (c + 1) * tile] = g
            cols = slice(c * tile, (c + 1) * tile)
            grad = lax.dot_general(
                gbuf[:, cols],
                vb[...],
                (((0,), (0,)), ((), ())),
                preferred_element_type=jnp.float32,
            )
            state = to_column(held_state[s, c])
            state = state + jnp.mean(grad * grad, axis=1, keepdims=True)
            new = c32[c] - (LEARNING * grad) * lax.rsqrt(state)
            state_row = to_row(state)

            @pl.when(s < steps - 1)
            def _():
                outgo[s + 1, c] = new.astype(jnp.bfloat16)
                out_state[s + 1, c] = state_row
                hop_copy(s + 1, c).start()
                state_copy(s + 1, c).start()

            @pl.when(s == steps - 1)
            def _():
                cout[c] = new
                csout[c] = state_row

        block = held[s].reshape(ctx_tiles * tile, -1)
        for r in range(row_tiles):
            rows = slice(r * tile, (r + 1) * tile)
            grad = jnp.dot(gbuf[rows, :], block, preferred_element_type=jnp.float32)
            state = vcol[rows, :] + jnp.mean(grad * grad, axis=1, keepdims=True)
            new = vout[rows, :] - (LEARNING * grad) * lax.rsqrt(state)
            vcol[rows, :] = state
            vout[rows, :] = new
            vb[rows, :] = new.astype(jnp.bfloat16)
        return 0

    lax.fori_loop(0, steps, one_stop, 0)

    for r in range(row_tiles):
        vsout[r : r + 1, :] = to_row(vcol[r * tile : (r + 1) * tile, :])

    for j in range(1, n_group):
        code_copy(j).wait_send()
    for stop in range(steps):
        for j in range(1, n_group):
            weight_copy(stop, j).wait_send()
    for stop in range(1, steps):
        for c in range(ctx_tiles):
            hop_copy(stop, c).wait_send()
            state_copy(stop, c).wait_send()


def body(
    n_group,
    n_blk,
    vertex,
    vertex_state,
    context,
    context_state,
    tile_weights,
    tile_rows,
    tile_cols,
    tile_counts,
    negatives,
):
    steps, cap, tile = tile_weights.shape[3], tile_weights.shape[4], tile_weights.shape[5]
    width = vertex.shape[1]
    row_tiles, ctx_tiles = vertex.shape[0] // tile, context.shape[0] // tile
    nneg = negatives.shape[-1]
    half = tile // SUB
    used = jnp.arange(cap)[None, None, :] < tile_counts[0, 0][..., None]
    codes = jnp.where(used, tile_cols[0, 0] * row_tiles + tile_rows[0, 0], -1)
    codes = jnp.broadcast_to(
        codes.reshape(n_group, steps * cap, 1, 1), (n_group, steps * cap, 1, tile)
    ).astype(jnp.float32)
    hits = negatives[0, 0][:, None, :, :] == jnp.arange(ctx_tiles)[None, :, None, None]
    negs = NEG_WEIGHT * jnp.sum(hits.astype(jnp.float32), axis=-1)
    negs = negs.reshape(steps, ctx_tiles * row_tiles)
    sizes = (n_group, n_blk, steps, cap, row_tiles, ctx_tiles, tile)
    vmem = pl.BlockSpec(memory_space=pltpu.VMEM)
    f32, bf16 = jnp.float32, jnp.bfloat16
    dma = pltpu.SemaphoreType.DMA
    vout, vsout, cout, csout = pl.pallas_call(
        functools.partial(kernel, sizes),
        out_shape=(
            jax.ShapeDtypeStruct((row_tiles * tile, width), f32),
            jax.ShapeDtypeStruct((row_tiles, tile), f32),
            jax.ShapeDtypeStruct((ctx_tiles, tile, width), f32),
            jax.ShapeDtypeStruct((ctx_tiles, 1, tile), f32),
        ),
        in_specs=[vmem] * 5
        + [pl.BlockSpec(memory_space=pltpu.SMEM), pl.BlockSpec(memory_space=pl.ANY)],
        out_specs=(vmem,) * 4,
        scratch_shapes=[
            pltpu.VMEM((row_tiles * tile, width), bf16),
            pltpu.VMEM((row_tiles * tile, 1), f32),
            pltpu.VMEM((steps, ctx_tiles, tile, width), bf16),
            pltpu.VMEM((steps, ctx_tiles, tile, width), bf16),
            pltpu.VMEM((steps, ctx_tiles, 1, tile), f32),
            pltpu.VMEM((steps, ctx_tiles, 1, tile), f32),
            pltpu.VMEM((ctx_tiles, tile, width), f32),
            pltpu.VMEM((row_tiles * tile, ctx_tiles * tile), bf16),
            pltpu.VMEM((row_tiles * ctx_tiles, tile, tile), bf16),
            pltpu.VMEM((steps, n_group, cap, half, SUB, tile), bf16),
            pltpu.VMEM((n_group, steps * cap, 1, tile), f32),
            pltpu.VMEM((n_group, steps * cap, SUB, tile), bf16),
            dma((steps, ctx_tiles)),
            dma((steps, ctx_tiles)),
            dma((steps, ctx_tiles)),
            dma((steps, ctx_tiles)),
            dma((steps, n_group)),
            dma((steps, n_group)),
            dma((n_group,)),
            dma((n_group,)),
            dma((steps,)),
            dma,
        ],
        compiler_params=pltpu.CompilerParams(
            collective_id=0, has_side_effects=True, vmem_limit_bytes=48 * 1024 * 1024
        ),
    )(
        vertex,
        vertex_state.reshape(row_tiles, tile),
        context.reshape(ctx_tiles, tile, width),
        context_state.reshape(ctx_tiles, 1, tile),
        codes,
        negs,
        tile_weights.reshape(n_group, steps, cap, half, SUB, tile),
    )
    return (
        vout,
        vsout.reshape(-1),
        cout.reshape(ctx_tiles * tile, width),
        csout.reshape(-1),
    )


def solution(mesh):
    in_specs = (
        P(("group", "blk"), None),
        P(("group", "blk")),
        P(("group", "blk"), None),
        P(("group", "blk")),
        P("group", "blk", None, None, None, None, None),
        P("group", "blk", None, None, None),
        P("group", "blk", None, None, None),
        P("group", "blk", None, None),
        P("group", "blk", None, None, None),
    )
    out_specs = (
        P(("group", "blk"), None),
        P(("group", "blk")),
        P(("group", "blk"), None),
        P(("group", "blk")),
    )
    step = functools.partial(body, mesh.shape["group"], mesh.shape["blk"])
    return jax.shard_map(step, mesh=mesh, in_specs=in_specs, out_specs=out_specs, check_vma=False)
```

profile of v0, /device:TPU:1, one launch (start us, length us, event | category | flops | bytes accessed | tf_op | source)
XLA Modules:
  0.0 63.8 jit_solution(2865642856704905894)
XLA Ops:
  0.6 0.1 lt.28
  0.7 0.7 %multiply_add_fusion = s32[1,1,4,6,3]{3,2,4,1,0:T(4,128)S(1)} fusion(s32[1,1,4,6,3]{3,2,4,1,0:T(4,128)} %param.14, s32[1,1,4,6,3]{3,2,4,1,0:T(4,128)} %param.15), kind=kLoop, calls=%fused_computation.3 | loop fusion | flops 144 | bytes 864 | tf_op jit(solution)/shard_map/add | solution.py:280
  1.4 0.1 copy.17
  1.5 0.1 add.13
  1.6 0.7 %convert_reduce_fusion = f32[6,4,8]{2,1,0:T(4,128)S(1)} fusion(s32[6,8,2]{1,2,0:T(2,128)} %bitcast.16), kind=kLoop, calls=%fused_computation | loop fusion | flops 960 | bytes 1152 | tf_op jit(solution)/shard_map/reduce_sum | solution.py:285
  2.4 0.1 mul.27.negs_ref
  2.4 0.8 %lt.31 = s32[4,6,3]{2,1,0:T(8,128)S(1)} broadcast(s32[4,6]{1,0:T(4,128)} %bitcast.17), dimensions={0,1} | broadcast | bytes 384 | tf_op jit(solution)/shard_map/lt | solution.py:279
  3.2 0.1 lt.32
  3.3 0.1 broadcast_in_dim.12.codes_ref
  3.4 0.0 copy-start
  3.4 1.7 %copy-done = bf16[1,1,4,6,3,128,128]{6,5,4,3,2,1,0:T(8,128)(2,1)S(1)} copy-done((bf16[1,1,4,6,3,128,128]{6,5,4,3,2,1,0:T(8,128)(2,1)S(1)}, bf16[1,1,4,6,3,128,128]{6,5,4,3,2,1,0:T(8,128)(2,1)}, u32[]{:S(2)}) %copy-start) | copy-done | bytes 2359320
  5.1 0.0 copy-start.1
  5.1 1.2 %copy-done.1 = f32[1024,256]{1,0:T(8,128)S(1)} copy-done((f32[1024,256]{1,0:T(8,128)S(1)}, f32[1024,256]{1,0:T(8,128)}, u32[]{:S(2)}) %copy-start.1) | copy-done | bytes 1048600
  6.3 0.0 copy-start.2
  6.3 1.0 %copy-done.2 = f32[512,256]{1,0:T(8,128)S(1)} copy-done((f32[512,256]{1,0:T(8,128)S(1)}, f32[512,256]{1,0:T(8,128)}, u32[]{:S(2)}) %copy-start.2) | copy-done | bytes 524312
  7.4 0.0 copy-start.3
  7.4 0.7 %copy-done.3 = f32[1024]{0:T(1024)S(1)} copy-done((f32[1024]{0:T(1024)S(1)}, f32[1024]{0:T(1024)}, u32[]{:S(2)}) %copy-start.3) | copy-done | bytes 4120
  8.0 0.0 copy-start.4
  8.0 0.7 %copy-done.4 = f32[512]{0:T(512)S(1)} copy-done((f32[512]{0:T(512)S(1)}, f32[512]{0:T(512)}, u32[]{:S(2)}) %copy-start.4) | copy-done | bytes 2072
  8.7 52.2 %shard_map.120 = (f32[1024,256]{1,0:T(8,128)S(1)}, f32[8,128]{1,0:T(8,128)S(1)}, f32[4,128,256]{2,1,0:T(8,128)S(1)}, f32[4,1,128]{2,1,0:T(1,128)S(1)}) custom-call(f32[1024,256]{1,0:T(8,128)S(1)} %copy-done.1, f32[8,128]{1,0:T(8,128)S(1)} %bitcast.13, f32[4,128,256]{2,1,0:T(8,128)S(1)} %bitcast.10, f32[4,1,128]{2,1,0:T(1,128)S(1)} %bitcast.14, ...), custom_call_target="tpu_custom_call" | custom-call | tf_op jit(solution)/shard_map/pallas_call | solution.py:291
  60.9 1.0 %copy.22 = f32[1024,256]{1,0:T(8,128)} copy(f32[1024,256]{1,0:T(8,128)S(1)} %get-tuple-element.16) | data formatting | bytes 2097152
  61.9 0.6 copy.23
  62.5 0.8 %copy.24 = f32[512,256]{1,0:T(8,128)} copy(f32[512,256]{1,0:T(8,128)S(1)} %bitcast.11) | data formatting | bytes 1048576
  63.2 0.6 copy.25
  (3 shorter events, 0.0 us)
Async XLA Ops:
  3.4 1.7 %copy-start = (bf16[1,1,4,6,3,128,128]{6,5,4,3,2,1,0:T(8,128)(2,1)S(1)}, bf16[1,1,4,6,3,128,128]{6,5,4,3,2,1,0:T(8,128)(2,1)}, u32[]{:S(2)}) copy-start(bf16[1,1,4,6,3,128,128]{6,5,4,3,2,1,0:T(8,128)(2,1)} %param.13) | copy-start | bytes 7077892
  5.1 1.2 %copy-start.1 = (f32[1024,256]{1,0:T(8,128)S(1)}, f32[1024,256]{1,0:T(8,128)}, u32[]{:S(2)}) copy-start(f32[1024,256]{1,0:T(8,128)} %vertex_ref.1) | copy-start | bytes 3145732
  6.3 1.0 %copy-start.2 = (f32[512,256]{1,0:T(8,128)S(1)}, f32[512,256]{1,0:T(8,128)}, u32[]{:S(2)}) copy-start(f32[512,256]{1,0:T(8,128)} %param.11) | copy-start | bytes 1572868
  7.4 0.7 %copy-start.3 = (f32[1024]{0:T(1024)S(1)}, f32[1024]{0:T(1024)}, u32[]{:S(2)}) copy-start(f32[1024]{0:T(1024)} %param.10) | copy-start | bytes 12292
  8.0 0.7 %copy-start.4 = (f32[512]{0:T(512)S(1)}, f32[512]{0:T(512)}, u32[]{:S(2)}) copy-start(f32[512]{0:T(512)} %param.12) | copy-start | bytes 6148
where the time goes:
time: 64.2 us; the launch traced here: 63.8 us
  Pallas kernels  52.2 us (81%)
  local copies, waits for them, and re-layouts  9.56 us (15%)
  other arithmetic  1.44 us (2%)
  between operations  0.68 us (1%)
    pallas_call x1, Pallas kernels, body(): pl.pallas_call(functools.partial(kernel, sizes), out_shape=(jax.ShapeDtyp...  52.2 us
    unnamed x14, local copies, waits for them, and re-layouts  8.23 us

commit v1 on v0

v1 whole, which is shorter than its diff:
```python
import functools

import jax
import jax.numpy as jnp
from jax import lax
from jax.experimental import pallas as pl
from jax.experimental.pallas import tpu as pltpu
from jax.sharding import PartitionSpec as P

LEARNING = 0.1
NEG_WEIGHT = 0.5
MESH = pl.DeviceIdType.MESH
VMEM_LIMIT = 54000000


def eye_mask(tile):
    return lax.broadcasted_iota(jnp.int32, (tile, tile), 0) == lax.broadcasted_iota(
        jnp.int32, (tile, tile), 1
    )


def to_column(row):
    tile = row.shape[1]
    return jnp.sum(jnp.where(eye_mask(tile), row, 0.0), axis=1, keepdims=True)


def to_row(column):
    tile = column.shape[0]
    return jnp.sum(jnp.where(eye_mask(tile), column, 0.0), axis=0, keepdims=True)


def kernel(
    sizes,
    codes_ref,
    negs_ref,
    vertex_hbm,
    vstate_hbm,
    context_hbm,
    cstate_hbm,
    weights_hbm,
    vout,
    vsout,
    cout,
    csout,
    vb,
    vcol,
    held,
    outgo,
    held_state,
    out_state,
    c32,
    gbuf,
    prefix,
    stage,
    wbuf,
    codebuf,
    plan_vmem,
    plan,
    hop_send,
    hop_recv,
    st_send,
    st_recv,
    w_send,
    w_recv,
    code_send,
    code_recv,
    own_sem,
    own_code_sem,
    in_sem,
    plan_sem,
):
    n_group, n_blk, steps, cap, row_tiles, ctx_tiles, tile = sizes
    slots = n_group * cap
    group = lax.axis_index("group")
    blk = lax.axis_index("blk")
    right = lax.rem(blk + 1, n_blk)
    left = lax.rem(blk + n_blk - 1, n_blk)

    def peer(j):
        return lax.rem(group + j, n_group)

    def code_copy(j):
        return pltpu.make_async_remote_copy(
            src_ref=codes_ref.at[:, peer(j)],
            dst_ref=codebuf.at[j],
            send_sem=code_send.at[j],
            recv_sem=code_recv.at[j],
            device_id={"group": peer(j)},
            device_id_type=MESH,
        )

    def weight_copy(stop, j):
        return pltpu.make_async_remote_copy(
            src_ref=weights_hbm.at[peer(j), stop],
            dst_ref=wbuf.at[pl.ds(stop * slots + j * cap, cap)],
            send_sem=w_send.at[stop, j],
            recv_sem=w_recv.at[stop, j],
            device_id={"group": peer(j)},
            device_id_type=MESH,
        )

    def own_copy(stop):
        return pltpu.make_async_copy(
            weights_hbm.at[group, stop],
            wbuf.at[pl.ds(stop * slots, cap)],
            own_sem.at[stop],
        )

    def own_code():
        return pltpu.make_async_copy(codes_ref.at[:, group], codebuf.at[0], own_code_sem)

    def hop_copy(stop, c):
        return pltpu.make_async_remote_copy(
            src_ref=outgo.at[stop, c],
            dst_ref=held.at[stop, c],
            send_sem=hop_send.at[stop, c],
            recv_sem=hop_recv.at[stop, c],
            device_id={"blk": right},
            device_id_type=MESH,
        )

    def state_copy(stop, c):
        return pltpu.make_async_remote_copy(
            src_ref=out_state.at[stop, c],
            dst_ref=held_state.at[stop, c],
            send_sem=st_send.at[stop, c],
            recv_sem=st_recv.at[stop, c],
            device_id={"blk": right},
            device_id_type=MESH,
        )

    barrier = pltpu.get_barrier_semaphore()
    pl.semaphore_signal(barrier, inc=1, device_id={"blk": left}, device_id_type=MESH)
    for j in range(1, n_group):
        pl.semaphore_signal(
            barrier, inc=1, device_id={"group": peer(j)}, device_id_type=MESH
        )
    vertex_in = pltpu.make_async_copy(vertex_hbm, vout, in_sem.at[0])
    context_in = pltpu.make_async_copy(context_hbm, c32, in_sem.at[1])
    vstate_in = pltpu.make_async_copy(vstate_hbm, vsout, in_sem.at[2])
    cstate_in = pltpu.make_async_copy(cstate_hbm, held_state.at[0], in_sem.at[3])
    vstate_in.start()
    cstate_in.start()
    context_in.start()
    vertex_in.start()
    own_code().start()
    for stop in range(steps):
        own_copy(stop).start()
    pl.semaphore_wait(barrier, n_group)

    for j in range(1, n_group):
        code_copy(j).start()
    for stop in range(steps):
        for j in range(1, n_group):
            weight_copy(stop, j).start()

    vstate_in.wait()
    cstate_in.wait()
    context_in.wait()
    vertex_in.wait()
    for r in range(row_tiles):
        rows = slice(r * tile, (r + 1) * tile)
        vb[rows, :] = vout[rows, :].astype(jnp.bfloat16)
        vcol[rows, :] = to_column(vsout[r : r + 1, :])
    for c in range(ctx_tiles):
        held[0, c] = c32[c].astype(jnp.bfloat16)

    own_code().wait()
    for j in range(1, n_group):
        code_copy(j).wait_recv()
    codes = [codebuf[j, k] for j in range(n_group) for k in range(cap)]
    lane = lax.broadcasted_iota(jnp.int32, codes[0].shape, 1)
    upto = jnp.zeros_like(lane)
    below = jnp.zeros_like(lane)
    order = jnp.zeros_like(lane)
    for n, code in enumerate(codes):
        upto = upto + jnp.where(code <= lane, 1, 0)
        below = below + jnp.where(code < lane, 1, 0)
        rank = jnp.zeros_like(lane)
        for m, other in enumerate(codes):
            if m < n:
                rank = rank + jnp.where(other <= code, 1, 0)
            elif m > n:
                rank = rank + jnp.where(other < code, 1, 0)
        order = order + jnp.where(rank == lane, n, 0)
    plan_vmem[0] = upto
    plan_vmem[1] = below
    plan_vmem[2] = order
    plan_copy = pltpu.make_async_copy(plan_vmem, plan, plan_sem)
    plan_copy.start()
    prefix[0] = jnp.zeros((tile, tile), jnp.float32)
    plan_copy.wait()

    def one_stop(s, _):
        own_copy(s).wait()
        for j in range(1, n_group):
            weight_copy(s, j).wait_recv()

        for n in range(slots):
            stage[n] = wbuf[s * slots + n]
        total = jnp.zeros((tile, tile), jnp.float32)
        for n in range(slots):
            total = total + stage[plan[2, s, n]].astype(jnp.float32)
            prefix[n + 1] = total

        for c in range(ctx_tiles):

            @pl.when(s > 0)
            def _():
                hop_copy(s, c).wait_recv()
                state_copy(s, c).wait_recv()
                c32[c] = held[s, c].astype(jnp.float32)

            ctx = held[s, c]
            cols = slice(c * tile, (c + 1) * tile)
            for r in range(row_tiles):
                rows = slice(r * tile, (r + 1) * tile)
                logits = lax.dot_general(
                    vb[rows, :],
                    ctx,
                    (((1,), (1,)), ((), ())),
                    preferred_element_type=jnp.float32,
                )
                pair = c * row_tiles + r
                negative = jnp.float32(0.0)
                for n in range(negs_ref.shape[1]):
                    negative = negative + jnp.where(negs_ref[s, n, r] == c, NEG_WEIGHT, 0.0)
                weight = prefix[plan[0, s, pair]] - prefix[plan[1, s, pair]]
                scale = 0.5 * weight + 0.5 * negative
                g = scale * jnp.tanh(0.5 * logits) + (scale - weight)
                gbuf[rows, cols] = g.astype(jnp.bfloat16)
            grad = lax.dot_general(
                gbuf[:, cols],
                vb[...],
                (((0,), (0,)), ((), ())),
                preferred_element_type=jnp.float32,
            )
            state = to_column(held_state[s, c])
            state = state + jnp.mean(grad * grad, axis=1, keepdims=True)
            new = c32[c] - grad * (LEARNING * lax.rsqrt(state))
            state_row = to_row(state)

            @pl.when(s < steps - 1)
            def _():
                outgo[s + 1, c] = new.astype(jnp.bfloat16)
                out_state[s + 1, c] = state_row
                hop_copy(s + 1, c).start()
                state_copy(s + 1, c).start()

            @pl.when(s == steps - 1)
            def _():
                cout[c] = new
                csout[c] = state_row

        block = held[s].reshape(ctx_tiles * tile, -1)
        for r in range(row_tiles):
            rows = slice(r * tile, (r + 1) * tile)
            grad = jnp.dot(gbuf[rows, :], block, preferred_element_type=jnp.float32)
            state = vcol[rows, :] + jnp.mean(grad * grad, axis=1, keepdims=True)
            new = vout[rows, :] - grad * (LEARNING * lax.rsqrt(state))
            vcol[rows, :] = state
            vout[rows, :] = new
            vb[rows, :] = new.astype(jnp.bfloat16)
        return 0

    lax.fori_loop(0, steps, one_stop, 0)

    for r in range(row_tiles):
        vsout[r : r + 1, :] = to_row(vcol[r * tile : (r + 1) * tile, :])

    for j in range(1, n_group):
        code_copy(j).wait_send()
    for stop in range(steps):
        for j in range(1, n_group):
            weight_copy(stop, j).wait_send()
    for stop in range(1, steps):
        for c in range(ctx_tiles):
            hop_copy(stop, c).wait_send()
            state_copy(stop, c).wait_send()


def put_out(*refs):
    count = len(refs) // 2
    sems = refs[-1]
    copies = [
        pltpu.make_async_copy(refs[i], refs[count + i], sems.at[i]) for i in range(count)
    ]
    for copy in copies:
        copy.start()
    for copy in copies:
        copy.wait()


def body(
    n_group,
    n_blk,
    vertex,
    vertex_state,
    context,
    context_state,
    tile_weights,
    tile_rows,
    tile_cols,
    tile_counts,
    negatives,
):
    steps, cap, tile = tile_weights.shape[3], tile_weights.shape[4], tile_weights.shape[5]
    width = vertex.shape[1]
    row_tiles, ctx_tiles = vertex.shape[0] // tile, context.shape[0] // tile
    pairs = row_tiles * ctx_tiles
    slots = n_group * cap
    assert pairs < tile and slots < tile

    def spread(ids):
        return jnp.broadcast_to(
            ids.transpose(2, 0, 1)[..., None], (cap, n_group, steps, tile)
        )

    used = (
        lax.broadcasted_iota(jnp.int32, (cap, n_group, steps, tile), 0)
        < tile_counts[0, 0][None, :, :, None]
    )
    codes = jnp.where(
        used, spread(tile_cols[0, 0]) * row_tiles + spread(tile_rows[0, 0]), pairs
    )
    sizes = (n_group, n_blk, steps, cap, row_tiles, ctx_tiles, tile)
    vmem = pl.BlockSpec(memory_space=pltpu.VMEM)
    hbm = pl.BlockSpec(memory_space=pltpu.HBM)
    f32, bf16 = jnp.float32, jnp.bfloat16
    dma = pltpu.SemaphoreType.DMA
    outs = (
        jax.ShapeDtypeStruct((row_tiles * tile, width), f32),
        jax.ShapeDtypeStruct((row_tiles, tile), f32),
        jax.ShapeDtypeStruct((ctx_tiles, tile, width), f32),
        jax.ShapeDtypeStruct((ctx_tiles, 1, tile), f32),
    )
    results = pl.pallas_call(
        functools.partial(kernel, sizes),
        out_shape=outs,
        in_specs=[vmem, pl.BlockSpec(memory_space=pltpu.SMEM)] + [hbm] * 5,
        out_specs=(vmem,) * 4,
        scratch_shapes=[
            pltpu.VMEM((row_tiles * tile, width), bf16),
            pltpu.VMEM((row_tiles * tile, 1), f32),
            pltpu.VMEM((steps, ctx_tiles, tile, width), bf16),
            pltpu.VMEM((steps, ctx_tiles, tile, width), bf16),
            pltpu.VMEM((steps, ctx_tiles, 1, tile), f32),
            pltpu.VMEM((steps, ctx_tiles, 1, tile), f32),
            pltpu.VMEM((ctx_tiles, tile, width), f32),
            pltpu.VMEM((row_tiles * tile, ctx_tiles * tile), bf16),
            pltpu.VMEM((slots + 1, tile, tile), f32),
            pltpu.VMEM((slots, tile, tile), bf16),
            pltpu.VMEM((steps * slots, tile, tile), bf16),
            pltpu.VMEM((n_group, cap, steps, tile), jnp.int32),
            pltpu.VMEM((3, steps, tile), jnp.int32),
            pltpu.SMEM((3, steps, tile), jnp.int32),
            dma((steps, ctx_tiles)),
            dma((steps, ctx_tiles)),
            dma((steps, ctx_tiles)),
            dma((steps, ctx_tiles)),
            dma((steps, n_group)),
            dma((steps, n_group)),
            dma((n_group,)),
            dma((n_group,)),
            dma((steps,)),
            dma,
            dma((4,)),
            dma,
        ],
        compiler_params=pltpu.CompilerParams(
            collective_id=0, has_side_effects=True, vmem_limit_bytes=VMEM_LIMIT
        ),
    )(
        codes,
        negatives[0, 0].transpose(0, 2, 1),
        vertex,
        vertex_state.reshape(row_tiles, tile),
        context.reshape(ctx_tiles, tile, width),
        context_state.reshape(ctx_tiles, 1, tile),
        tile_weights.reshape(n_group, steps, cap, tile, tile),
    )
    vout, vsout, cout, csout = pl.pallas_call(
        put_out,
        out_shape=outs,
        in_specs=[vmem] * 4,
        out_specs=(hbm,) * 4,
        scratch_shapes=[dma((4,))],
        compiler_params=pltpu.CompilerParams(vmem_limit_bytes=1024 * 1024),
    )(*results)
    return (
        vout,
        vsout.reshape(-1),
        cout.reshape(ctx_tiles * tile, width),
        csout.reshape(-1),
    )


def solution(mesh):
    in_specs = (
        P(("group", "blk"), None),
        P(("group", "blk")),
        P(("group", "blk"), None),
        P(("group", "blk")),
        P("group", "blk", None, None, None, None, None),
        P("group", "blk", None, None, None),
        P("group", "blk", None, None, None),
        P("group", "blk", None, None),
        P("group", "blk", None, None, None),
    )
    out_specs = (
        P(("group", "blk"), None),
        P(("group", "blk")),
        P(("group", "blk"), None),
        P(("group", "blk")),
    )
    step = functools.partial(body, mesh.shape["group"], mesh.shape["blk"])
    return jax.shard_map(step, mesh=mesh, in_specs=in_specs, out_specs=out_specs, check_vma=False)
```

time: 64.2 us -> 53.3 us (0.83)
  local copies, waits for them, and re-layouts: 9.56 us -> 3.1 us
  Pallas kernels: 52.2 us -> 47.7 us
    unnamed x14 -> x8, local copies, waits for them, and re-layouts: 8.23 us -> 3.1 us
    pallas_call x1 -> x2, Pallas kernels: 52.2 us -> 47.7 us  [the longest x1 46.5 us: body(): pl.pallas_call(functools.partial(kernel, sizes), out_shape=outs, in_specs...]
    lt x4 -> x0, local copies, waits for them, and re-layouts: 0.91 us -> none  [body(): used = jnp.arange(cap)[None, None, :] < tile_counts[0, 0][..., None]]
    select_n x0 -> x1, other arithmetic: none -> 0.76 us  [body(): jnp.where(used, spread(tile_cols[0, 0]) * row_tiles + spread(tile_rows[0,...]
    reduce_sum x1 -> x0, other arithmetic: 0.71 us -> none  [body(): negs = NEG_WEIGHT * jnp.sum(hits.astype(jnp.float32), axis=-1)]
where the time goes in v1:
time: 53.3 us; the launch traced here: 53 us
  Pallas kernels  47.7 us (89%)
  local copies, waits for them, and re-layouts  3.1 us (6%)
  other arithmetic  1.47 us (3%)
  between operations  0.66 us (1%)
    pallas_call x1, Pallas kernels, body(): pl.pallas_call(functools.partial(kernel, sizes), out_shape=outs, in_specs...  46.5 us
    unnamed x8, local copies, waits for them, and re-layouts  3.1 us
    pallas_call x1, Pallas kernels, body(): pl.pallas_call(put_out, out_shape=outs, in_specs=[vmem] * 4, out_specs=(h...  1.18 us

profile of v1, /device:TPU:1, one launch (start us, length us, event | category | flops | bytes accessed | tf_op | source)
XLA Modules:
  0.0 53.0 jit_solution(3995772701129845644)
XLA Ops:
  0.6 0.7 %add_bitcast_fusion = s32[3,4,6]{2,1,0:T(4,128)S(1)} fusion(s32[1,1,4,6,3]{3,2,4,1,0:T(4,128)} %param.14, s32[1,1,4,6,3]{3,2,4,1,0:T(4,128)} %param.15), kind=kLoop, calls=%fused_computation.2 | loop fusion | flops 144 | bytes 864 | tf_op jit(solution)/shard_map/add | solution.py:324
  1.3 0.8 %fusion.codes_ref = s32[3,4,6,128]{3,2,1,0:T(8,128)S(1)} fusion(s32[3,4,6]{2,1,0:T(4,128)S(1)} %add_bitcast_fusion, s32[4,6]{1,0:T(4,128)} %bitcast.20), kind=kLoop, calls=%fused_computation.1 | loop fusion | flops 18432 | bytes 37248 | tf_op jit(solution)/shard_map/jit(_where)/select_n | solution.py:323
  2.1 0.0 copy-start
  2.1 1.0 %copy-done = f32[512,256]{1,0:T(8,128)S(1)} copy-done((f32[512,256]{1,0:T(8,128)S(1)}, f32[512,256]{1,0:T(8,128)}, u32[]{:S(2)}) %copy-start) | copy-done | bytes 524312
  3.2 0.0 copy-start.1
  3.2 0.7 %copy-done.1 = s32[1,1,6,8,2]{3,4,2,1,0:T(2,128)S(1)} copy-done((s32[1,1,6,8,2]{3,4,2,1,0:T(2,128)S(1)}, s32[1,1,6,8,2]{3,4,2,1,0:T(2,128)}, u32[]{:S(2)}) %copy-start.1) | copy-done | bytes 408
  3.8 0.0 copy-start.2
  3.8 0.7 %copy-done.2 = f32[1024]{0:T(1024)S(1)} copy-done((f32[1024]{0:T(1024)S(1)}, f32[1024]{0:T(1024)}, u32[]{:S(2)}) %copy-start.2) | copy-done | bytes 4120
  4.5 0.0 copy-start.3
  4.5 0.7 %copy-done.3 = f32[512]{0:T(512)S(1)} copy-done((f32[512]{0:T(512)S(1)}, f32[512]{0:T(512)}, u32[]{:S(2)}) %copy-start.3) | copy-done | bytes 2072
  5.2 46.5 %shard_map.120 = (f32[1024,256]{1,0:T(8,128)S(1)}, f32[8,128]{1,0:T(8,128)S(1)}, f32[4,128,256]{2,1,0:T(8,128)S(1)}, f32[4,1,128]{2,1,0:T(1,128)S(1)}) custom-call(s32[3,4,6,128]{3,2,1,0:T(8,128)S(1)} %fusion.codes_ref, s32[6,2,8]{2,1,0:T(2,128)S(1)} %bitcast.16, f32[1024,256]{1,0:T(8,128)} %vertex_hbm.1, f32[8,128]{1,0:T(8,128)S(1)} %bitcast.17, ...), custom_call_target="tpu_custom_call" | custom-call | tf_op jit(solution)/shard_map/pallas_call | solution.py:337
  51.8 1.2 %shard_map.121 = (f32[1024,256]{1,0:T(8,128)}, f32[8,128]{1,0:T(8,128)}, f32[4,128,256]{2,1,0:T(8,128)}, f32[4,1,128]{2,1,0:T(1,128)}) custom-call(f32[1024,256]{1,0:T(8,128)S(1)} %get-tuple-element.12.refs_0_, f32[8,128]{1,0:T(8,128)S(1)} %get-tuple-element.13.refs_1_, f32[4,128,256]{2,1,0:T(8,128)S(1)} %get-tuple-element.14.refs_2_, ...), custom_call_target="tpu_custom_call" | custom-call | tf_op jit(solution)/shard_map/pallas_call | solution.py:382
Async XLA Ops:
  2.1 1.0 %copy-start = (f32[512,256]{1,0:T(8,128)S(1)}, f32[512,256]{1,0:T(8,128)}, u32[]{:S(2)}) copy-start(f32[512,256]{1,0:T(8,128)} %param.11) | copy-start | bytes 1572868
  3.2 0.7 %copy-start.1 = (s32[1,1,6,8,2]{3,4,2,1,0:T(2,128)S(1)}, s32[1,1,6,8,2]{3,4,2,1,0:T(2,128)}, u32[]{:S(2)}) copy-start(s32[1,1,6,8,2]{3,4,2,1,0:T(2,128)} %param.17) | copy-start | bytes 1156
  3.8 0.7 %copy-start.2 = (f32[1024]{0:T(1024)S(1)}, f32[1024]{0:T(1024)}, u32[]{:S(2)}) copy-start(f32[1024]{0:T(1024)} %param.10) | copy-start | bytes 12292
  4.5 0.7 %copy-start.3 = (f32[512]{0:T(512)S(1)}, f32[512]{0:T(512)}, u32[]{:S(2)}) copy-start(f32[512]{0:T(512)} %param.12) | copy-start | bytes 6148

commit v2 on v1

--- a/solution.py
+++ b/solution.py
@@ -161,7 +161,7 @@
     for r in range(row_tiles):
         rows = slice(r * tile, (r + 1) * tile)
         vb[rows, :] = vout[rows, :].astype(jnp.bfloat16)
-        vcol[rows, :] = to_column(vsout[r : r + 1, :])
+        vcol[rows, :] = jnp.broadcast_to(to_column(vsout[r : r + 1, :]), (tile, tile))
     for c in range(ctx_tiles):
         held[0, c] = c32[c].astype(jnp.bfloat16)
 
@@ -191,7 +191,19 @@
     prefix[0] = jnp.zeros((tile, tile), jnp.float32)
     plan_copy.wait()
 
-    def one_stop(s, _):
+    width = vb.shape[1]
+    batch = 2 if ctx_tiles % 2 == 0 else 1
+    spread_mean = jnp.full((width, tile), 1.0 / width, jnp.bfloat16)
+
+    def wide(value):
+        return jnp.concatenate([value] * (width // tile), axis=1)
+
+    def mean_square(grad):
+        return jnp.dot(
+            (grad * grad).astype(jnp.bfloat16), spread_mean, preferred_element_type=jnp.float32
+        )
+
+    def one_stop(s, first, last):
         own_copy(s).wait()
         for j in range(1, n_group):
             weight_copy(s, j).wait_recv()
@@ -200,70 +212,85 @@
             stage[n] = wbuf[s * slots + n]
         total = jnp.zeros((tile, tile), jnp.float32)
         for n in range(slots):
-            total = total + stage[plan[2, s, n]].astype(jnp.float32)
+            total = total + 0.5 * stage[plan[2, s, n]].astype(jnp.float32)
             prefix[n + 1] = total
 
-        for c in range(ctx_tiles):
-
-            @pl.when(s > 0)
-            def _():
-                hop_copy(s, c).wait_recv()
-                state_copy(s, c).wait_recv()
-                c32[c] = held[s, c].astype(jnp.float32)
-
-            ctx = held[s, c]
-            cols = slice(c * tile, (c + 1) * tile)
+        def pair_gradients(first_tile):
+            tiles = range(first_tile, first_tile + batch)
+            if not first:
+                for c in tiles:
+                    hop_copy(s, c).wait_recv()
+                    state_copy(s, c).wait_recv()
+            ctx = held[s, first_tile : first_tile + batch].reshape(batch * tile, width)
+            half_logits = lax.dot_general(
+                vb[...],
+                ctx * jnp.bfloat16(0.5),
+                (((1,), (1,)), ((), ())),
+                preferred_element_type=jnp.float32,
+            )
             for r in range(row_tiles):
                 rows = slice(r * tile, (r + 1) * tile)
-                logits = lax.dot_general(
-                    vb[rows, :],
-                    ctx,
-                    (((1,), (1,)), ((), ())),
-                    preferred_element_type=jnp.float32,
-                )
-                pair = c * row_tiles + r
-                negative = jnp.float32(0.0)
-                for n in range(negs_ref.shape[1]):
-                    negative = negative + jnp.where(negs_ref[s, n, r] == c, NEG_WEIGHT, 0.0)
-                weight = prefix[plan[0, s, pair]] - prefix[plan[1, s, pair]]
-                scale = 0.5 * weight + 0.5 * negative
-                g = scale * jnp.tanh(0.5 * logits) + (scale - weight)
-                gbuf[rows, cols] = g.astype(jnp.bfloat16)
-            grad = lax.dot_general(
-                gbuf[:, cols],
+                for i, c in enumerate(tiles):
+                    pair = c * row_tiles + r
+                    negative = jnp.float32(0.0)
+                    for n in range(negs_ref.shape[1]):
+                        negative = negative + jnp.where(
+                            negs_ref[s, n, r] == c, 0.5 * NEG_WEIGHT, 0.0
+                        )
+                    weight = prefix[plan[0, s, pair]] - prefix[plan[1, s, pair]]
+                    part = half_logits[rows, i * tile : (i + 1) * tile]
+                    g = (negative + weight) * jnp.tanh(part) + (negative - weight)
+                    gbuf[rows, c * tile : (c + 1) * tile] = g.astype(jnp.bfloat16)
+
+        def context_update(first_tile):
+            grads = lax.dot_general(
+                gbuf[:, first_tile * tile : (first_tile + batch) * tile],
                 vb[...],
                 (((0,), (0,)), ((), ())),
                 preferred_element_type=jnp.float32,
             )
-            state = to_column(held_state[s, c])
-            state = state + jnp.mean(grad * grad, axis=1, keepdims=True)
-            new = c32[c] - grad * (LEARNING * lax.rsqrt(state))
-            state_row = to_row(state)
-
-            @pl.when(s < steps - 1)
-            def _():
-                outgo[s + 1, c] = new.astype(jnp.bfloat16)
-                out_state[s + 1, c] = state_row
-                hop_copy(s + 1, c).start()
-                state_copy(s + 1, c).start()
-
-            @pl.when(s == steps - 1)
-            def _():
-                cout[c] = new
-                csout[c] = state_row
-
-        block = held[s].reshape(ctx_tiles * tile, -1)
-        for r in range(row_tiles):
-            rows = slice(r * tile, (r + 1) * tile)
-            grad = jnp.dot(gbuf[rows, :], block, preferred_element_type=jnp.float32)
-            state = vcol[rows, :] + jnp.mean(grad * grad, axis=1, keepdims=True)
-            new = vout[rows, :] - grad * (LEARNING * lax.rsqrt(state))
-            vcol[rows, :] = state
-            vout[rows, :] = new
-            vb[rows, :] = new.astype(jnp.bfloat16)
+            means = mean_square(grads)
+            for i in range(batch):
+                c = first_tile + i
+                part = slice(i * tile, (i + 1) * tile)
+                before = jnp.broadcast_to(to_column(held_state[s, c]), (tile, tile))
+                state = before + means[part]
+                old = c32[c] if first else held[s, c].astype(jnp.float32)
+                new = old - grads[part] * wide(LEARNING * lax.rsqrt(state))
+                state_row = to_row(state)
+                if last:
+                    cout[c] = new
+                    csout[c] = state_row
+                else:
+                    outgo[s + 1, c] = new.astype(jnp.bfloat16)
+                    out_state[s + 1, c] = state_row
+                    hop_copy(s + 1, c).start()
+                    state_copy(s + 1, c).start()
+
+        for c in range(0, ctx_tiles, batch):
+            pair_gradients(c)
+            context_update(c)
+
+        block = held[s].reshape(ctx_tiles * tile, width)
+        half = row_tiles // 2
+        for h in range(2):
+            span = slice(h * half * tile, (h + 1) * half * tile)
+            grads = jnp.dot(gbuf[span, :], block, preferred_element_type=jnp.float32)
+            state = vcol[span, :] + mean_square(grads)
+            new = vout[span, :] - grads * wide(LEARNING * lax.rsqrt(state))
+            vcol[span, :] = state
+            vout[span, :] = new
+            vb[span, :] = new.astype(jnp.bfloat16)
+
+    def middle_stop(s, _):
+        one_stop(s, False, False)
         return 0
 
-    lax.fori_loop(0, steps, one_stop, 0)
+    one_stop(0, True, steps == 1)
+    if steps > 2:
+        lax.fori_loop(1, steps - 1, middle_stop, 0)
+    if steps > 1:
+        one_stop(steps - 1, False, True)
 
     for r in range(row_tiles):
         vsout[r : r + 1, :] = to_row(vcol[r * tile : (r + 1) * tile, :])
@@ -341,7 +368,7 @@
         out_specs=(vmem,) * 4,
         scratch_shapes=[
             pltpu.VMEM((row_tiles * tile, width), bf16),
-            pltpu.VMEM((row_tiles * tile, 1), f32),
+            pltpu.VMEM((row_tiles * tile, tile), f32),
             pltpu.VMEM((steps, ctx_tiles, tile, width), bf16),
             pltpu.VMEM((steps, ctx_tiles, tile, width), bf16),
             pltpu.VMEM((steps, ctx_tiles, 1, tile), f32),

time: 53.3 us -> 54.3 us (1.019)
  the two profiles are of different devices: /device:TPU:1 before, /device:TPU:0 now
where the time goes in v2:
time: 54.3 us; the launch traced here: 53.9 us
  Pallas kernels  48.7 us (90%)
  local copies, waits for them, and re-layouts  3.1 us (6%)
  other arithmetic  1.47 us (3%)
  between operations  0.66 us (1%)
    pallas_call x1, Pallas kernels, body(): pl.pallas_call(functools.partial(kernel, sizes), out_shape=outs, in_specs...  47.5 us
    unnamed x8, local copies, waits for them, and re-layouts  3.1 us
    pallas_call x1, Pallas kernels, body(): pl.pallas_call(put_out, out_shape=outs, in_specs=[vmem] * 4, out_specs=(h...  1.18 us

profile of v2, /device:TPU:0, one launch (start us, length us, event | category | flops | bytes accessed | tf_op | source)
XLA Modules:
  0.0 53.9 jit_solution(1158968150458310076)
XLA Ops:
  0.6 0.7 %add_bitcast_fusion = s32[3,4,6]{2,1,0:T(4,128)S(1)} fusion(s32[1,1,4,6,3]{3,2,4,1,0:T(4,128)} %param.14, s32[1,1,4,6,3]{3,2,4,1,0:T(4,128)} %param.15), kind=kLoop, calls=%fused_computation.2 | loop fusion | flops 144 | bytes 864 | tf_op jit(solution)/shard_map/add | solution.py:351
  1.3 0.8 %fusion.codes_ref = s32[3,4,6,128]{3,2,1,0:T(8,128)S(1)} fusion(s32[3,4,6]{2,1,0:T(4,128)S(1)} %add_bitcast_fusion, s32[4,6]{1,0:T(4,128)} %bitcast.20), kind=kLoop, calls=%fused_computation.1 | loop fusion | flops 18432 | bytes 37248 | tf_op jit(solution)/shard_map/jit(_where)/select_n | solution.py:350
  2.1 0.0 copy-start
  2.1 1.0 %copy-done = f32[512,256]{1,0:T(8,128)S(1)} copy-done((f32[512,256]{1,0:T(8,128)S(1)}, f32[512,256]{1,0:T(8,128)}, u32[]{:S(2)}) %copy-start) | copy-done | bytes 524312
  3.2 0.0 copy-start.1
  3.2 0.7 %copy-done.1 = s32[1,1,6,8,2]{3,4,2,1,0:T(2,128)S(1)} copy-done((s32[1,1,6,8,2]{3,4,2,1,0:T(2,128)S(1)}, s32[1,1,6,8,2]{3,4,2,1,0:T(2,128)}, u32[]{:S(2)}) %copy-start.1) | copy-done | bytes 408
  3.8 0.0 copy-start.2
  3.8 0.7 %copy-done.2 = f32[1024]{0:T(1024)S(1)} copy-done((f32[1024]{0:T(1024)S(1)}, f32[1024]{0:T(1024)}, u32[]{:S(2)}) %copy-start.2) | copy-done | bytes 4120
  4.5 0.0 copy-start.3
  4.5 0.7 %copy-done.3 = f32[512]{0:T(512)S(1)} copy-done((f32[512]{0:T(512)S(1)}, f32[512]{0:T(512)}, u32[]{:S(2)}) %copy-start.3) | copy-done | bytes 2072
  5.2 47.5 %shard_map.120 = (f32[1024,256]{1,0:T(8,128)S(1)}, f32[8,128]{1,0:T(8,128)S(1)}, f32[4,128,256]{2,1,0:T(8,128)S(1)}, f32[4,1,128]{2,1,0:T(1,128)S(1)}) custom-call(s32[3,4,6,128]{3,2,1,0:T(8,128)S(1)} %fusion.codes_ref, s32[6,2,8]{2,1,0:T(2,128)S(1)} %bitcast.16, f32[1024,256]{1,0:T(8,128)} %vertex_hbm.1, f32[8,128]{1,0:T(8,128)S(1)} %bitcast.17, ...), custom_call_target="tpu_custom_call" | custom-call | tf_op jit(solution)/shard_map/pallas_call | solution.py:364
  52.7 1.2 %shard_map.121 = (f32[1024,256]{1,0:T(8,128)}, f32[8,128]{1,0:T(8,128)}, f32[4,128,256]{2,1,0:T(8,128)}, f32[4,1,128]{2,1,0:T(1,128)}) custom-call(f32[1024,256]{1,0:T(8,128)S(1)} %get-tuple-element.12.refs_0_, f32[8,128]{1,0:T(8,128)S(1)} %get-tuple-element.13.refs_1_, f32[4,128,256]{2,1,0:T(8,128)S(1)} %get-tuple-element.14.refs_2_, ...), custom_call_target="tpu_custom_call" | custom-call | tf_op jit(solution)/shard_map/pallas_call | solution.py:409
Async XLA Ops:
  2.1 1.0 %copy-start = (f32[512,256]{1,0:T(8,128)S(1)}, f32[512,256]{1,0:T(8,128)}, u32[]{:S(2)}) copy-start(f32[512,256]{1,0:T(8,128)} %param.11) | copy-start | bytes 1572868
  3.2 0.7 %copy-start.1 = (s32[1,1,6,8,2]{3,4,2,1,0:T(2,128)S(1)}, s32[1,1,6,8,2]{3,4,2,1,0:T(2,128)}, u32[]{:S(2)}) copy-start(s32[1,1,6,8,2]{3,4,2,1,0:T(2,128)} %param.17) | copy-start | bytes 1156
  3.8 0.7 %copy-start.2 = (f32[1024]{0:T(1024)S(1)}, f32[1024]{0:T(1024)}, u32[]{:S(2)}) copy-start(f32[1024]{0:T(1024)} %param.10) | copy-start | bytes 12292
  4.5 0.7 %copy-start.3 = (f32[512]{0:T(512)S(1)}, f32[512]{0:T(512)}, u32[]{:S(2)}) copy-start(f32[512]{0:T(512)} %param.12) | copy-start | bytes 6148

commit v3 on v2

--- a/solution.py
+++ b/solution.py
@@ -192,7 +192,7 @@
     plan_copy.wait()
 
     width = vb.shape[1]
-    batch = 2 if ctx_tiles % 2 == 0 else 1
+    batch = 1
     spread_mean = jnp.full((width, tile), 1.0 / width, jnp.bfloat16)
 
     def wide(value):

time: 54.3 us -> 53.1 us (0.978)
  the two profiles are of different devices: /device:TPU:0 before, /device:TPU:1 now
where the time goes in v3:
time: 53.1 us; the launch traced here: 52.8 us
  Pallas kernels  47.6 us (90%)
  local copies, waits for them, and re-layouts  3.1 us (6%)
  other arithmetic  1.47 us (3%)
  between operations  0.66 us (1%)
    pallas_call x1, Pallas kernels, body(): pl.pallas_call(functools.partial(kernel, sizes), out_shape=outs, in_specs...  46.4 us
    unnamed x8, local copies, waits for them, and re-layouts  3.1 us
    pallas_call x1, Pallas kernels, body(): pl.pallas_call(put_out, out_shape=outs, in_specs=[vmem] * 4, out_specs=(h...  1.18 us

profile of v3, /device:TPU:1, one launch (start us, length us, event | category | flops | bytes accessed | tf_op | source)
XLA Modules:
  0.0 52.8 jit_solution(16860680930847084495)
XLA Ops:
  0.6 0.7 %add_bitcast_fusion = s32[3,4,6]{2,1,0:T(4,128)S(1)} fusion(s32[1,1,4,6,3]{3,2,4,1,0:T(4,128)} %param.14, s32[1,1,4,6,3]{3,2,4,1,0:T(4,128)} %param.15), kind=kLoop, calls=%fused_computation.2 | loop fusion | flops 144 | bytes 864 | tf_op jit(solution)/shard_map/add | solution.py:351
  1.3 0.8 %fusion.codes_ref = s32[3,4,6,128]{3,2,1,0:T(8,128)S(1)} fusion(s32[3,4,6]{2,1,0:T(4,128)S(1)} %add_bitcast_fusion, s32[4,6]{1,0:T(4,128)} %bitcast.20), kind=kLoop, calls=%fused_computation.1 | loop fusion | flops 18432 | bytes 37248 | tf_op jit(solution)/shard_map/jit(_where)/select_n | solution.py:350
  2.1 0.0 copy-start
  2.1 1.0 %copy-done = f32[512,256]{1,0:T(8,128)S(1)} copy-done((f32[512,256]{1,0:T(8,128)S(1)}, f32[512,256]{1,0:T(8,128)}, u32[]{:S(2)}) %copy-start) | copy-done | bytes 524312
  3.2 0.0 copy-start.1
  3.2 0.7 %copy-done.1 = s32[1,1,6,8,2]{3,4,2,1,0:T(2,128)S(1)} copy-done((s32[1,1,6,8,2]{3,4,2,1,0:T(2,128)S(1)}, s32[1,1,6,8,2]{3,4,2,1,0:T(2,128)}, u32[]{:S(2)}) %copy-start.1) | copy-done | bytes 408
  3.8 0.0 copy-start.2
  3.8 0.7 %copy-done.2 = f32[1024]{0:T(1024)S(1)} copy-done((f32[1024]{0:T(1024)S(1)}, f32[1024]{0:T(1024)}, u32[]{:S(2)}) %copy-start.2) | copy-done | bytes 4120
  4.5 0.0 copy-start.3
  4.5 0.7 %copy-done.3 = f32[512]{0:T(512)S(1)} copy-done((f32[512]{0:T(512)S(1)}, f32[512]{0:T(512)}, u32[]{:S(2)}) %copy-start.3) | copy-done | bytes 2072
  5.2 46.4 %shard_map.120 = (f32[1024,256]{1,0:T(8,128)S(1)}, f32[8,128]{1,0:T(8,128)S(1)}, f32[4,128,256]{2,1,0:T(8,128)S(1)}, f32[4,1,128]{2,1,0:T(1,128)S(1)}) custom-call(s32[3,4,6,128]{3,2,1,0:T(8,128)S(1)} %fusion.codes_ref, s32[6,2,8]{2,1,0:T(2,128)S(1)} %bitcast.16, f32[1024,256]{1,0:T(8,128)} %vertex_hbm.1, f32[8,128]{1,0:T(8,128)S(1)} %bitcast.17, ...), custom_call_target="tpu_custom_call" | custom-call | tf_op jit(solution)/shard_map/pallas_call | solution.py:364
  51.6 1.2 %shard_map.121 = (f32[1024,256]{1,0:T(8,128)}, f32[8,128]{1,0:T(8,128)}, f32[4,128,256]{2,1,0:T(8,128)}, f32[4,1,128]{2,1,0:T(1,128)}) custom-call(f32[1024,256]{1,0:T(8,128)S(1)} %get-tuple-element.12.refs_0_, f32[8,128]{1,0:T(8,128)S(1)} %get-tuple-element.13.refs_1_, f32[4,128,256]{2,1,0:T(8,128)S(1)} %get-tuple-element.14.refs_2_, ...), custom_call_target="tpu_custom_call" | custom-call | tf_op jit(solution)/shard_map/pallas_call | solution.py:409
Async XLA Ops:
  2.1 1.0 %copy-start = (f32[512,256]{1,0:T(8,128)S(1)}, f32[512,256]{1,0:T(8,128)}, u32[]{:S(2)}) copy-start(f32[512,256]{1,0:T(8,128)} %param.11) | copy-start | bytes 1572868
  3.2 0.7 %copy-start.1 = (s32[1,1,6,8,2]{3,4,2,1,0:T(2,128)S(1)}, s32[1,1,6,8,2]{3,4,2,1,0:T(2,128)}, u32[]{:S(2)}) copy-start(s32[1,1,6,8,2]{3,4,2,1,0:T(2,128)} %param.17) | copy-start | bytes 1156
  3.8 0.7 %copy-start.2 = (f32[1024]{0:T(1024)S(1)}, f32[1024]{0:T(1024)}, u32[]{:S(2)}) copy-start(f32[1024]{0:T(1024)} %param.10) | copy-start | bytes 12292
  4.5 0.7 %copy-start.3 = (f32[512]{0:T(512)S(1)}, f32[512]{0:T(512)}, u32[]{:S(2)}) copy-start(f32[512]{0:T(512)} %param.12) | copy-start | bytes 6148
